TPU v7x, 32 devices: a whole 2x2x4 slice. The times are simulated.
32 devices in a mesh: vec: 16 (over z, y, x), row: 2 (over core).
Axes of the slice: x: 2, y: 2, z: 4, core: 2. Of those that a mesh axis runs over, the one named last changes fastest.
Arguments:
- vectors: bfloat16 [2, 4096, 1024], P('row', 'vec'), may hold values from -6 to 6
- rotation: bfloat16 [1024, 1024], P(None, 'vec'), may hold values from -0.1875 to 0.1875
- blocks: bfloat16 [64, 8, 128, 128], P('row'), may hold values from -0.125 to 0.125
- column_blocks: int32 [64, 8], P('row'), may hold values from -2 to 65, as said below
Outputs:
- filtered: bfloat16 [2, 4096, 1024], P('row', 'vec')
Inputs may be any that keep to these rules, and one draw needn't show every extreme that they name: `column_blocks`: block row r of partition p = r // 32 lists 8 distinct column blocks between p * 32 - 2 and p * 32 + 33; the first block row of every partition lists the lowest of these and the last one the highest; column blocks outside 0 to 63 stand for zeros.
All inputs are finite; a program needn't handle non-finite values.
Results may differ from a plain program's by a relative error of at most 0.006.
Values may be sent and summed in bfloat16 or wider, within the bound.
No kernel may reach another device: no remote copies, remote signals or barrier semaphores. Data moves between devices by JAX's collectives and lax.ppermute only.
A program may use at most 64 MiB of HBM per device.

v0:
```python
import jax
import jax.numpy as jnp
from jax import lax
from jax.sharding import PartitionSpec as P

BS = 128
HB = 2
STEPS = 4
centre = 0.3
half_width = 1.2


def with_halo(block, sides, width):
    for axis, dim in sides:
        count = lax.axis_size(axis)
        forward = [(i, i + 1) for i in range(count - 1)]
        backward = [(target, source) for source, target in forward]
        low = lax.ppermute(
            lax.slice_in_dim(block, block.shape[dim] - width, None, axis=dim), axis, forward
        )
        high = lax.ppermute(lax.slice_in_dim(block, 0, width, axis=dim), axis, backward)
        block = jnp.concatenate([low, block, high], axis=dim)
    return block


def apply_matrix(operand, blocks, offsets):
    extended = with_halo(operand, (("row", 1),), HB * BS)
    stacked = extended.reshape(extended.shape[0], -1, BS)
    picked = stacked[:, offsets]
    product = jnp.einsum("rjab,krjb->kra", blocks, picked, preferred_element_type=jnp.float32)
    return product.reshape(extended.shape[0], -1)


def filter_panel(vec_panel, blocks, offsets):
    previous = vec_panel.astype(jnp.float32)
    current = (apply_matrix(vec_panel, blocks, offsets) - centre * previous) / half_width
    for turn_index in range(STEPS - 1):
        operand = current.astype(jnp.bfloat16)
        following = (
            2.0 * (apply_matrix(operand, blocks, offsets) - centre * current) / half_width
            - previous
        )
        previous = current
        current = following
    return current.astype(jnp.bfloat16)


def local(vectors, rotation, blocks, column_blocks):
    local_rows = vectors[0]
    offsets = column_blocks - (lax.axis_index("row") * column_blocks.shape[0] - HB)
    contract = (((0,), (1,)), ((), ()))
    rotated = lax.dot_general(
        lax.all_gather(rotation, "vec", axis=1, tiled=True),
        local_rows,
        contract,
        preferred_element_type=jnp.float32,
    ).astype(jnp.bfloat16)
    vec_panel = lax.all_to_all(rotated, "vec", split_axis=0, concat_axis=1, tiled=True)
    filtered = filter_panel(vec_panel, blocks, offsets)
    returned = lax.all_to_all(filtered, "vec", split_axis=1, concat_axis=0, tiled=True)
    return jnp.transpose(returned)[None]


def solution(mesh):
    placed = (P("row", "vec", None), P(None, "vec"), P("row", None, None, None), P("row", None))
    return jax.shard_map(
        local, mesh=mesh, in_specs=placed, out_specs=P("row", "vec", None), check_vma=False
    )
```

profile of v0, /device:TPU:0, one launch (start us, length us, event | category | flops | bytes accessed | tf_op | source)
XLA Modules:
  0.0 203.2 jit_solution(18180730329563429137)
XLA Ops:
  6.5 0.7 all-gather.2.cloned.1.call-update
  7.3 66.0 %all-gather.2.cloned.1.call-done = bf16[1024,1024]{0,1:T(8,128)(2,1)} async-done(((bf16[1024,64]{0,1:T(8,128)(2,1)}), bf16[1024,1024]{0,1:T(8,128)(2,1)}) %all-gather.2.cloned.1.call-update) | async-done | bytes 2097168 | tf_op jit(solution)/shard_map/all_gather | solution.py:53
  73.2 3.1 %convolution_convert_fusion = bf16[1024,256]{1,0:T(8,128)(2,1)} fusion(bf16[1024,1024]{0,1:T(8,128)(2,1)} %all-gather.2.cloned.1.call-done, bf16[1,256,1024]{2,1,0:T(8,128)(2,1)S(1)} %copy-done), kind=kOutput, calls=%fused_computation.9 | convolution fusion | flops 537133056 | bytes 3145728 | tf_op jit(solution)/shard_map/dot_general | solution.py:52
  76.4 4.4 %all-to-all-start = ((bf16[16,64,256]{2,1,0:T(8,128)(2,1)}), bf16[16,64,256]{2,1,0:T(8,128)(2,1)S(1)}, u32[]{:S(2)}, u32[]{:S(2)}) async-start(bf16[16,64,256]{2,1,0:T(8,128)(2,1)} %bitcast.1), calls=%async_computation | async-start | bytes 1048576 | tf_op jit(solution)/shard_map/all_to_all | solution.py:58
  80.8 0.1 copy.22
  80.9 0.1 reshape.53
  81.0 14.0 %all-to-all-done = bf16[16,64,256]{2,1,0:T(8,128)(2,1)S(1)} async-done(((bf16[16,64,256]{2,1,0:T(8,128)(2,1)}), bf16[16,64,256]{2,1,0:T(8,128)(2,1)S(1)}, u32[]{:S(2)}, u32[]{:S(2)}) %all-to-all-start) | async-done | bytes 524320 | tf_op jit(solution)/shard_map/all_to_all | solution.py:58
  95.0 0.0 copy-start.1
  95.0 1.3 collective-permute-start
  96.3 1.3 collective-permute-start.1
  97.7 0.0 collective-permute-done
  97.7 1.8 collective-permute-done.1
  99.4 0.2 copy_bitcast_fusion.3
  99.6 3.0 %gather_fusion = bf16[256,64,128]{2,1,0:T(8,128)(2,1)} fusion(bf16[64,36,128]{2,0,1:T(8,128)(2,1)S(1)} %copy_bitcast_fusion.3, s32[1024]{0:T(1024)S(1)} %pad_clamp_fusion), kind=kCustom, calls=%fused_computation | custom fusion | bytes 8389632 | tf_op jit(solution)/shard_map/gather | solution.py:29
  102.7 7.6 %fusion.12 = f32[32,64,128,1]{2,1,3,0:T(8,128)S(1)} fusion(bf16[64,32,8,128]{3,0,2,1:T(8,128)(2,1)} %bitcast.117, bf16[32,8,128,128]{3,2,1,0:T(8,128)(2,1)} %param.6), kind=kOutput, calls=%fused_computation.36 | convolution fusion | flops 536870912 | bytes 13631488 | tf_op jit(solution)/shard_map/rjab,krjb->kra/dot_general | solution.py:30
  110.3 0.2 multiply_convert_fusion
  110.5 2.1 %collective-permute-start.2 = (bf16[64,256]{1,0:T(8,128)(2,1)S(1)}, bf16[64,256]{1,0:T(8,128)(2,1)S(1)}, u32[]{:S(2)}, u32[]{:S(2)}) collective-permute-start(bf16[64,256]{1,0:T(8,128)(2,1)S(1)} %get-tuple-element.9), channel_id=1, source_target_pairs={{0,1},{2,3},{4,5},{6,7},{8,9},{10,11},{12,13},{14,15},{16,17},{18,... | collective-permute-start | bytes 98312 | tf_op jit(solution)/shard_map/ppermute | solution.py:18
  112.5 1.3 collective-permute-start.3
  113.8 1.8 collective-permute-done.3
  115.6 0.2 copy_bitcast_fusion.2
  115.8 3.0 %gather_fusion.1 = bf16[256,64,128]{2,1,0:T(8,128)(2,1)} fusion(bf16[64,36,128]{2,0,1:T(8,128)(2,1)S(1)} %copy_bitcast_fusion.2, s32[1024]{0:T(1024)S(1)} %pad_clamp_fusion), kind=kCustom, calls=%fused_computation.1 | custom fusion | bytes 8389632 | tf_op jit(solution)/shard_map/gather | solution.py:29
  118.8 7.6 %fusion.13 = f32[32,64,128,1]{2,1,3,0:T(8,128)S(1)} fusion(bf16[64,32,8,128]{3,0,2,1:T(8,128)(2,1)} %bitcast.118, bf16[32,8,128,128]{3,2,1,0:T(8,128)(2,1)} %param.6), kind=kOutput, calls=%fused_computation.37 | convolution fusion | flops 536870912 | bytes 13631488 | tf_op jit(solution)/shard_map/rjab,krjb->kra/dot_general | solution.py:30
  126.5 0.3 fusion.7
  126.8 2.1 %collective-permute-start.4 = (bf16[64,256]{1,0:T(8,128)(2,1)S(1)}, bf16[64,256]{1,0:T(8,128)(2,1)S(1)}, u32[]{:S(2)}, u32[]{:S(2)}) collective-permute-start(bf16[64,256]{1,0:T(8,128)(2,1)S(1)} %get-tuple-element.7), channel_id=1, source_target_pairs={{0,1},{2,3},{4,5},{6,7},{8,9},{10,11},{12,13},{14,15},{16,17},{18,... | collective-permute-start | bytes 98312 | tf_op jit(solution)/shard_map/ppermute | solution.py:18
  128.9 1.3 collective-permute-start.5
  130.2 1.8 collective-permute-done.5
  132.0 0.2 copy_bitcast_fusion.1
  132.1 3.0 %gather_fusion.2 = bf16[256,64,128]{2,1,0:T(8,128)(2,1)} fusion(bf16[64,36,128]{2,0,1:T(8,128)(2,1)S(1)} %copy_bitcast_fusion.1, s32[1024]{0:T(1024)S(1)} %pad_clamp_fusion), kind=kCustom, calls=%fused_computation.2 | custom fusion | bytes 8389632 | tf_op jit(solution)/shard_map/gather | solution.py:29
  135.2 7.6 %fusion.14 = f32[32,64,128,1]{2,1,3,0:T(8,128)S(1)} fusion(bf16[64,32,8,128]{3,0,2,1:T(8,128)(2,1)} %bitcast.119, bf16[32,8,128,128]{3,2,1,0:T(8,128)(2,1)} %param.6), kind=kOutput, calls=%fused_computation.38 | convolution fusion | flops 536870912 | bytes 13631488 | tf_op jit(solution)/shard_map/rjab,krjb->kra/dot_general | solution.py:30
  142.8 0.5 fusion.4
  143.3 0.5 copy-done.4
  143.8 2.1 %collective-permute-start.6 = (bf16[64,256]{1,0:T(8,128)(2,1)S(1)}, bf16[64,256]{1,0:T(8,128)(2,1)S(1)}, u32[]{:S(2)}, u32[]{:S(2)}) collective-permute-start(bf16[64,256]{1,0:T(8,128)(2,1)S(1)} %get-tuple-element.5), channel_id=1, source_target_pairs={{0,1},{2,3},{4,5},{6,7},{8,9},{10,11},{12,13},{14,15},{16,17},{18,... | collective-permute-start | bytes 98312 | tf_op jit(solution)/shard_map/ppermute | solution.py:18
  145.9 1.5 collective-permute-start.7
  147.4 1.6 copy.24
  149.0 2.6 %reshape.50 = f32[64,16,256]{2,1,0:T(8,128)} reshape(f32[64,32,128]{2,1,0:T(8,128)} %copy.24) | data formatting | bytes 2097152 | tf_op jit(solution)/shard_map/reshape | solution.py:31
  151.6 1.6 copy.26
  153.2 1.5 reshape.49
  154.7 1.6 copy.28
  156.3 2.5 %reshape.48 = f32[64,16,256]{2,1,0:T(8,128)} reshape(f32[64,32,128]{2,1,0:T(8,128)} %copy.28) | data formatting | bytes 2097152 | tf_op jit(solution)/shard_map/reshape | solution.py:31
  158.9 0.2 copy_bitcast_fusion
  159.0 3.0 %gather_fusion.3 = bf16[256,64,128]{2,1,0:T(8,128)(2,1)} fusion(bf16[64,36,128]{2,0,1:T(8,128)(2,1)S(1)} %copy_bitcast_fusion, s32[1024]{0:T(1024)S(1)} %pad_clamp_fusion), kind=kCustom, calls=%fused_computation.3 | custom fusion | bytes 8389632 | tf_op jit(solution)/shard_map/gather | solution.py:29
  162.1 7.6 %convolution_bitcast_fusion = f32[64,32,128]{2,0,1:T(8,128)S(1)} fusion(bf16[64,32,8,128]{3,0,2,1:T(8,128)(2,1)} %bitcast.116, bf16[32,8,128,128]{3,2,1,0:T(8,128)(2,1)} %param.6), kind=kOutput, calls=%fused_computation.4 | convolution fusion | flops 536870912 | bytes 13631488 | tf_op jit(solution)/shard_map/rjab,krjb->kra/dot_general | solution.py:30
  169.7 1.6 copy.30
  171.3 2.5 %reshape.47 = f32[64,16,256]{2,1,0:T(8,128)} reshape(f32[64,32,128]{2,1,0:T(8,128)} %copy.30) | data formatting | bytes 2097152 | tf_op jit(solution)/shard_map/reshape | solution.py:31
  173.8 2.4 %subtract_convert_fusion = bf16[64,16,256]{2,1,0:T(8,128)(2,1)S(1)} fusion(f32[64,16,256]{2,1,0:T(8,128)} %reshape.47, f32[64,16,256]{2,1,0:T(8,128)} %reshape.48, f32[64,16,256]{2,1,0:T(8,128)S(1)} %reshape.49, f32[64,16,256]{2,1,0:T(8,128)S(1)} %copy-done.8, bf16[16,64,256]{2,1,0:T(8,128)(2,1)S(1)} %copy-done.7), kind=kLoop, calls=%fused_computation.18 | loop fusion | flops 4456448 | bytes 5242880 | tf_op jit(solution)/shard_map/convert_element_type | solution.py:45
  176.2 0.2 copy.34
  176.3 19.0 %all_to_all.35 = bf16[64,16,256]{2,0,1:T(8,128)(2,1)S(1)} all-to-all(bf16[64,16,256]{2,0,1:T(8,128)(2,1)S(1)} %copy.34), channel_id=1, replica_groups=mesh['vec'=16,'row'=2] {'vec'}, dimensions={1} | all-to-all | bytes 1048576 | tf_op jit(solution)/shard_map/all_to_all | solution.py:60
  195.3 1.0 copy.35
  (34 shorter events, 0.1 us)
Async XLA Ops:
  6.5 66.7 %copy-start = (bf16[1,256,1024]{2,1,0:T(8,128)(2,1)S(1)}, bf16[1,256,1024]{2,1,0:T(8,128)(2,1)}, u32[]{:S(2)}) copy-start(bf16[1,256,1024]{2,1,0:T(8,128)(2,1)} %param.4) | copy-start | bytes 1572868
  6.5 74.3 %copy-start.11 = (s32[32,8]{0,1:T(8,128)S(1)}, s32[32,8]{0,1:T(8,128)}, u32[]{:S(2)}) copy-start(s32[32,8]{0,1:T(8,128)} %param.7) | copy-start | bytes 3076
  6.5 66.7 %all-gather.2.cloned.1.call-start = ((), (), s32[]{:S(2)}) async-start(), calls=%async_computation.2 | async-start | bytes 2228224 | tf_op jit(solution)/shard_map/all_gather | solution.py:53
  76.4 18.6 %all-to-all-start = ((bf16[16,64,256]{2,1,0:T(8,128)(2,1)}), bf16[16,64,256]{2,1,0:T(8,128)(2,1)S(1)}, u32[]{:S(2)}, u32[]{:S(2)}) async-start(bf16[16,64,256]{2,1,0:T(8,128)(2,1)} %bitcast.1), calls=%async_computation | async-start | bytes 1048576 | tf_op jit(solution)/shard_map/all_to_all | solution.py:58
  95.0 2.7 %copy-start.6 = (bf16[16,64,256]{2,1,0:T(8,128)(2,1)}, bf16[16,64,256]{2,1,0:T(8,128)(2,1)S(1)}, u32[]{:S(2)}) copy-start(bf16[16,64,256]{2,1,0:T(8,128)(2,1)S(1)} %all-to-all-done) | copy-start | bytes 1572868
  95.0 15.2 %copy-start.1 = (bf16[8,8,16,256]{3,1,2,0:T(8,128)(2,1)}, bf16[8,8,16,256]{3,1,2,0:T(8,128)(2,1)S(1)}, u32[]{:S(2)}) copy-start(bf16[8,8,16,256]{3,1,2,0:T(8,128)(2,1)S(1)} %copy.47) | copy-start | bytes 1572868
  95.0 2.6 %collective-permute-start = (bf16[64,256]{1,0:T(8,128)(2,1)S(1)}, bf16[64,256]{1,0:T(8,128)(2,1)S(1)}, u32[]{:S(2)}, u32[]{:S(2)}) collective-permute-start(bf16[64,256]{1,0:T(8,128)(2,1)S(1)} %get-tuple-element.11), channel_id=1, source_target_pairs={{0,1},{2,3},{4,5},{6,7},{8,9},{10,11},{12,13},{14,15},{16,17},{18,... | collective-permute-start | bytes 98312 | tf_op jit(solution)/shard_map/ppermute | solution.py:18
  96.3 3.1 %collective-permute-start.1 = (bf16[64,256]{1,0:T(8,128)(2,1)S(1)}, bf16[64,256]{1,0:T(8,128)(2,1)S(1)}, u32[]{:S(2)}, u32[]{:S(2)}) collective-permute-start(bf16[64,256]{1,0:T(8,128)(2,1)S(1)} %get-tuple-element.12), channel_id=1, source_target_pairs={{1,0},{3,2},{5,4},{7,6},{9,8},{11,10},{13,12},{15,14},{17,16},{19,... | collective-permute-start | bytes 98312 | tf_op jit(solution)/shard_map/ppermute | solution.py:21
  110.5 3.4 %collective-permute-start.2 = (bf16[64,256]{1,0:T(8,128)(2,1)S(1)}, bf16[64,256]{1,0:T(8,128)(2,1)S(1)}, u32[]{:S(2)}, u32[]{:S(2)}) collective-permute-start(bf16[64,256]{1,0:T(8,128)(2,1)S(1)} %get-tuple-element.9), channel_id=1, source_target_pairs={{0,1},{2,3},{4,5},{6,7},{8,9},{10,11},{12,13},{14,15},{16,17},{18,... | collective-permute-start | bytes 98312 | tf_op jit(solution)/shard_map/ppermute | solution.py:18
  112.5 3.1 %collective-permute-start.3 = (bf16[64,256]{1,0:T(8,128)(2,1)S(1)}, bf16[64,256]{1,0:T(8,128)(2,1)S(1)}, u32[]{:S(2)}, u32[]{:S(2)}) collective-permute-start(bf16[64,256]{1,0:T(8,128)(2,1)S(1)} %get-tuple-element.10), channel_id=1, source_target_pairs={{1,0},{3,2},{5,4},{7,6},{9,8},{11,10},{13,12},{15,14},{17,16},{19,... | collective-permute-start | bytes 98312 | tf_op jit(solution)/shard_map/ppermute | solution.py:21
  118.8 7.7 %copy-start.2 = (bf16[8,8,16,256]{3,1,2,0:T(8,128)(2,1)S(1)}, bf16[8,8,16,256]{3,1,2,0:T(8,128)(2,1)}, u32[]{:S(2)}) copy-start(bf16[8,8,16,256]{3,1,2,0:T(8,128)(2,1)} %copy-done.1) | copy-start | bytes 1572868
  126.8 3.4 %collective-permute-start.4 = (bf16[64,256]{1,0:T(8,128)(2,1)S(1)}, bf16[64,256]{1,0:T(8,128)(2,1)S(1)}, u32[]{:S(2)}, u32[]{:S(2)}) collective-permute-start(bf16[64,256]{1,0:T(8,128)(2,1)S(1)} %get-tuple-element.7), channel_id=1, source_target_pairs={{0,1},{2,3},{4,5},{6,7},{8,9},{10,11},{12,13},{14,15},{16,17},{18,... | collective-permute-start | bytes 98312 | tf_op jit(solution)/shard_map/ppermute | solution.py:18
  128.9 3.1 %collective-permute-start.5 = (bf16[64,256]{1,0:T(8,128)(2,1)S(1)}, bf16[64,256]{1,0:T(8,128)(2,1)S(1)}, u32[]{:S(2)}, u32[]{:S(2)}) collective-permute-start(bf16[64,256]{1,0:T(8,128)(2,1)S(1)} %get-tuple-element.8), channel_id=1, source_target_pairs={{1,0},{3,2},{5,4},{7,6},{9,8},{11,10},{13,12},{15,14},{17,16},{19,... | collective-permute-start | bytes 98312 | tf_op jit(solution)/shard_map/ppermute | solution.py:21
  135.2 7.7 %copy-start.3 = (bf16[8,8,16,256]{3,1,2,0:T(8,128)(2,1)S(1)}, bf16[8,8,16,256]{3,1,2,0:T(8,128)(2,1)}, u32[]{:S(2)}) copy-start(bf16[8,8,16,256]{3,1,2,0:T(8,128)(2,1)} %copy-done.1) | copy-start | bytes 1572868
  142.8 1.0 copy-start.4
  143.8 3.6 %copy-start.9 = (bf16[64,4096]{1,0:T(8,128)(2,1)}, bf16[64,4096]{1,0:T(8,128)(2,1)S(1)}, u32[]{:S(2)}) copy-start(bf16[64,4096]{1,0:T(8,128)(2,1)S(1)} %fusion.4) | copy-start | bytes 1572868
  143.8 15.0 %collective-permute-start.6 = (bf16[64,256]{1,0:T(8,128)(2,1)S(1)}, bf16[64,256]{1,0:T(8,128)(2,1)S(1)}, u32[]{:S(2)}, u32[]{:S(2)}) collective-permute-start(bf16[64,256]{1,0:T(8,128)(2,1)S(1)} %get-tuple-element.5), channel_id=1, source_target_pairs={{0,1},{2,3},{4,5},{6,7},{8,9},{10,11},{12,13},{14,15},{16,17},{18,... | collective-permute-start | bytes 98312 | tf_op jit(solution)/shard_map/ppermute | solution.py:18
  145.9 12.9 %collective-permute-start.7 = (bf16[64,256]{1,0:T(8,128)(2,1)S(1)}, bf16[64,256]{1,0:T(8,128)(2,1)S(1)}, u32[]{:S(2)}, u32[]{:S(2)}) collective-permute-start(bf16[64,256]{1,0:T(8,128)(2,1)S(1)} %get-tuple-element.6), channel_id=1, source_target_pairs={{1,0},{3,2},{5,4},{7,6},{9,8},{11,10},{13,12},{15,14},{17,16},{19,... | collective-permute-start | bytes 98312 | tf_op jit(solution)/shard_map/ppermute | solution.py:21
  149.0 5.7 %copy-start.5 = (f32[32,64,128,1]{2,1,3,0:T(8,128)S(1)}, f32[32,64,128,1]{2,1,3,0:T(8,128)}, u32[]{:S(2)}) copy-start(f32[32,64,128,1]{2,1,3,0:T(8,128)} %copy-done.4) | copy-start | bytes 3145732
  151.6 7.2 %copy-start.10 = (bf16[64,4096]{1,0:T(8,128)(2,1)S(1)}, bf16[64,4096]{1,0:T(8,128)(2,1)}, u32[]{:S(2)}) copy-start(bf16[64,4096]{1,0:T(8,128)(2,1)} %copy-done.9) | copy-start | bytes 1572868
  169.7 4.1 %copy-start.7 = (bf16[16,64,256]{2,1,0:T(8,128)(2,1)S(1)}, bf16[16,64,256]{2,1,0:T(8,128)(2,1)}, u32[]{:S(2)}) copy-start(bf16[16,64,256]{2,1,0:T(8,128)(2,1)} %copy-done.6) | copy-start | bytes 1572868
  169.7 4.1 %copy-start.8 = (f32[64,16,256]{2,1,0:T(8,128)S(1)}, f32[64,16,256]{2,1,0:T(8,128)}, u32[]{:S(2)}) copy-start(f32[64,16,256]{2,1,0:T(8,128)} %reshape.50) | copy-start | bytes 3145732
Sparse Core Ops, SparseCore 0:
  10.1 63.0 all-gather.1
where the time goes:
time: 204 us; the launch traced here: 203 us
  waiting for transfers between devices  86 us (42%)
  matrix products  33.6 us (16%)
  local copies, waits for them, and re-layouts  29.7 us (15%)
  blocking collectives  19 us (9%)
  starting transfers between devices  17.3 us (8%)
  between operations  13.7 us (7%)
  other arithmetic  3.9 us (2%)
    all_gather x1, waiting for transfers between devices, local(): lax.all_gather(rotation, 'vec', axis=1, tiled=True)  66 us
    dot_general x4, matrix products, apply_matrix(): jnp.einsum('rjab,krjb->kra', blocks, picked, preferred_element_type=jnp.f...  30.5 us
    all_to_all x1, blocking collectives, local(): lax.all_to_all(filtered, 'vec', split_axis=1, concat_axis=0, tiled=True)  19 us
    all_to_all x1, waiting for transfers between devices, local(): lax.all_to_all(rotated, 'vec', split_axis=0, concat_axis=1, tiled=True)  14 us
    gather x4, local copies, waits for them, and re-layouts, apply_matrix(): picked = stacked[:, offsets]  12.2 us
    reshape x4, local copies, waits for them, and re-layouts, apply_matrix(): return product.reshape(extended.shape[0], -1)  9.18 us
    ppermute x4, starting transfers between devices, with_halo(): lax.ppermute(lax.slice_in_dim(block, block.shape[dim] - width, None, axis...  7.49 us
    transpose x4, local copies, waits for them, and re-layouts, apply_matrix(): jnp.einsum('rjab,krjb->kra', blocks, picked, preferred_element_type=jnp.f...  6.33 us
  transfers between devices with their start and end apart: 10, of which 5 were waited for; matrix products, arithmetic and copies ran while one was open for 6% of the time, Pallas kernels for 0%

commit v1 on v0

--- a/solution.py
+++ b/solution.py
@@ -8,6 +8,22 @@
 STEPS = 4
 centre = 0.3
 half_width = 1.2
+
+
+def collect(x, axis, dim):
+    ways, here, step = (lax.axis_size(axis), lax.axis_index(axis), x.shape[dim])
+    shape = [n * ways if d == dim else n for d, n in enumerate(x.shape)]
+    full = lax.dynamic_update_slice_in_dim(jnp.zeros(shape, x.dtype), x, here * step, axis=dim)
+    going_up = going_down = x
+    for far in range(1, ways // 2 + 1):
+        going_up = lax.ppermute(going_up, axis, [(d, (d + 1) % ways) for d in range(ways)])
+        full = lax.dynamic_update_slice_in_dim(full, going_up, (here - far) % ways * step, axis=dim)
+        if 2 * far < ways:
+            going_down = lax.ppermute(going_down, axis, [(d, (d - 1) % ways) for d in range(ways)])
+            full = lax.dynamic_update_slice_in_dim(
+                full, going_down, (here + far) % ways * step, axis=dim
+            )
+    return full
 
 
 def with_halo(block, sides, width):
@@ -50,10 +66,7 @@
     offsets = column_blocks - (lax.axis_index("row") * column_blocks.shape[0] - HB)
     contract = (((0,), (1,)), ((), ()))
     rotated = lax.dot_general(
-        lax.all_gather(rotation, "vec", axis=1, tiled=True),
-        local_rows,
-        contract,
-        preferred_element_type=jnp.float32,
+        collect(rotation, "vec", 1), local_rows, contract, preferred_element_type=jnp.float32
     ).astype(jnp.bfloat16)
     vec_panel = lax.all_to_all(rotated, "vec", split_axis=0, concat_axis=1, tiled=True)
     filtered = filter_panel(vec_panel, blocks, offsets)

time: 204 us -> 191 us (0.936)
  starting transfers between devices: 17.3 us -> 57.7 us
  waiting for transfers between devices: 86 us -> 46.6 us
  between operations: 13.7 us -> 0.49 us
    all_gather x1 -> x0, waiting for transfers between devices: 66 us -> none  [local(): lax.all_gather(rotation, 'vec', axis=1, tiled=True)]
    ppermute x0 -> x15, starting transfers between devices: none -> 41.3 us  [the longest x7 38.3 us: collect(): lax.ppermute(going_down, axis, [(d, (d - 1) % ways) for d in range(ways)])]
    ppermute x0 -> x15, waiting for transfers between devices: none -> 30.7 us  [the longest x8 30.5 us: collect(): lax.ppermute(going_up, axis, [(d, (d + 1) % ways) for d in range(ways)])]
    all_to_all x1, waiting for transfers between devices: 14 us -> 10.5 us  [local(): lax.all_to_all(rotated, 'vec', split_axis=0, concat_axis=1, tiled=True)]
  transfers between devices with their start and end apart: 10 -> 24, of which waited for: 5 -> 13; matrix products, arithmetic and copies ran while one was open for 6% -> 6% of each run, Pallas kernels for 0% -> 0%
where the time goes in v1:
time: 191 us
  starting transfers between devices  57.7 us (30%)
  waiting for transfers between devices  46.6 us (24%)
  matrix products  32 us (17%)
  local copies, waits for them, and re-layouts  30.9 us (16%)
  blocking collectives  19.1 us (10%)
  other arithmetic  3.9 us (2%)
    ppermute x7, starting transfers between devices, collect(): lax.ppermute(going_down, axis, [(d, (d - 1) % ways) for d in range(ways)])  38.3 us
    dot_general x4, matrix products, apply_matrix(): jnp.einsum('rjab,krjb->kra', blocks, picked, preferred_element_type=jnp.f...  30.5 us
    ppermute x8, waiting for transfers between devices, collect(): lax.ppermute(going_up, axis, [(d, (d + 1) % ways) for d in range(ways)])  30.5 us
    all_to_all x1, blocking collectives, local(): lax.all_to_all(filtered, 'vec', split_axis=1, concat_axis=0, tiled=True)  19.1 us
    gather x4, local copies, waits for them, and re-layouts, apply_matrix(): picked = stacked[:, offsets]  12.3 us
    all_to_all x1, waiting for transfers between devices, local(): lax.all_to_all(rotated, 'vec', split_axis=0, concat_axis=1, tiled=True)  10.5 us
    reshape x4, local copies, waits for them, and re-layouts, apply_matrix(): return product.reshape(extended.shape[0], -1)  9.09 us
    ppermute x4, starting transfers between devices, with_halo(): lax.ppermute(lax.slice_in_dim(block, block.shape[dim] - width, None, axis...  7.48 us
  transfers between devices with their start and end apart: 24, of which 13 were waited for; matrix products, arithmetic and copies ran while one was open for 6% of the time, Pallas kernels for 0%

profile of v1, /device:TPU:0, one launch (start us, length us, event | category | flops | bytes accessed | tf_op | source)
XLA Modules:
  0.0 190.8 jit_solution(6429857822969243766)
XLA Ops:
  0.0 3.0 %collective-permute-start = (bf16[1024,64]{0,1:T(8,128)(2,1)}, bf16[1024,64]{0,1:T(8,128)(2,1)S(1)}, u32[]{:S(2)}, u32[]{:S(2)}) collective-permute-start(bf16[1024,64]{0,1:T(8,128)(2,1)} %param.5), channel_id=1, source_target_pairs={{0,2},{2,4},{4,6},{6,8},{8,10},{10,12},{12,14},{14,16},{16,18},{18... | collective-permute-start | bytes 393224 | tf_op jit(solution)/shard_map/ppermute | solution.py:19
  3.0 4.1 %collective-permute-start.1 = (bf16[1024,64]{0,1:T(8,128)(2,1)}, bf16[1024,64]{0,1:T(8,128)(2,1)S(1)}, u32[]{:S(2)}, u32[]{:S(2)}) collective-permute-start(bf16[1024,64]{0,1:T(8,128)(2,1)} %param.5), channel_id=1, source_target_pairs={{0,30},{2,0},{4,2},{6,4},{8,6},{10,8},{12,10},{14,12},{16,14},{18,... | collective-permute-start | bytes 393224 | tf_op jit(solution)/shard_map/ppermute | solution.py:22
  7.3 3.5 %collective-permute-done = bf16[1024,64]{0,1:T(8,128)(2,1)S(1)} collective-permute-done((bf16[1024,64]{0,1:T(8,128)(2,1)}, bf16[1024,64]{0,1:T(8,128)(2,1)S(1)}, u32[]{:S(2)}, u32[]{:S(2)}) %collective-permute-start) | collective-permute-done | bytes 131104 | tf_op jit(solution)/shard_map/ppermute | solution.py:19
  11.0 5.4 %collective-permute-start.3 = (bf16[1024,64]{0,1:T(8,128)(2,1)S(1)}, bf16[1024,64]{0,1:T(8,128)(2,1)S(1)}, u32[]{:S(2)}, u32[]{:S(2)}) collective-permute-start(bf16[1024,64]{0,1:T(8,128)(2,1)S(1)} %collective-permute-done.1), channel_id=1, source_target_pairs={{0,30},{2,0},{4,2},{6,4},{8,6},{10,8},{12,10},{14,12},{16,14},{18,... | collective-permute-start | bytes 393224 | tf_op jit(solution)/shard_map/ppermute | solution.py:22
  16.5 2.9 %collective-permute-done.2 = bf16[1024,64]{0,1:T(8,128)(2,1)S(1)} collective-permute-done((bf16[1024,64]{0,1:T(8,128)(2,1)S(1)}, bf16[1024,64]{0,1:T(8,128)(2,1)S(1)}, u32[]{:S(2)}, u32[]{:S(2)}) %collective-permute-start.2) | collective-permute-done | bytes 131104 | tf_op jit(solution)/shard_map/ppermute | solution.py:19
  19.4 5.7 %collective-permute-start.5 = (bf16[1024,64]{0,1:T(8,128)(2,1)S(1)}, bf16[1024,64]{0,1:T(8,128)(2,1)S(1)}, u32[]{:S(2)}, u32[]{:S(2)}) collective-permute-start(bf16[1024,64]{0,1:T(8,128)(2,1)S(1)} %collective-permute-done.3), channel_id=1, source_target_pairs={{0,30},{2,0},{4,2},{6,4},{8,6},{10,8},{12,10},{14,12},{16,14},{18,... | collective-permute-start | bytes 393224 | tf_op jit(solution)/shard_map/ppermute | solution.py:22
  25.1 2.9 %collective-permute-done.4 = bf16[1024,64]{0,1:T(8,128)(2,1)S(1)} collective-permute-done((bf16[1024,64]{0,1:T(8,128)(2,1)S(1)}, bf16[1024,64]{0,1:T(8,128)(2,1)S(1)}, u32[]{:S(2)}, u32[]{:S(2)}) %collective-permute-start.4) | collective-permute-done | bytes 131104 | tf_op jit(solution)/shard_map/ppermute | solution.py:19
  28.0 5.7 %collective-permute-start.7 = (bf16[1024,64]{0,1:T(8,128)(2,1)S(1)}, bf16[1024,64]{0,1:T(8,128)(2,1)S(1)}, u32[]{:S(2)}, u32[]{:S(2)}) collective-permute-start(bf16[1024,64]{0,1:T(8,128)(2,1)S(1)} %collective-permute-done.5), channel_id=1, source_target_pairs={{0,30},{2,0},{4,2},{6,4},{8,6},{10,8},{12,10},{14,12},{16,14},{18,... | collective-permute-start | bytes 393224 | tf_op jit(solution)/shard_map/ppermute | solution.py:22
  33.8 2.9 %collective-permute-done.6 = bf16[1024,64]{0,1:T(8,128)(2,1)S(1)} collective-permute-done((bf16[1024,64]{0,1:T(8,128)(2,1)S(1)}, bf16[1024,64]{0,1:T(8,128)(2,1)S(1)}, u32[]{:S(2)}, u32[]{:S(2)}) %collective-permute-start.6) | collective-permute-done | bytes 131104 | tf_op jit(solution)/shard_map/ppermute | solution.py:19
  36.7 5.6 %collective-permute-start.9 = (bf16[1024,64]{0,1:T(8,128)(2,1)S(1)}, bf16[1024,64]{0,1:T(8,128)(2,1)S(1)}, u32[]{:S(2)}, u32[]{:S(2)}) collective-permute-start(bf16[1024,64]{0,1:T(8,128)(2,1)S(1)} %collective-permute-done.7), channel_id=1, source_target_pairs={{0,30},{2,0},{4,2},{6,4},{8,6},{10,8},{12,10},{14,12},{16,14},{18,... | collective-permute-start | bytes 393224 | tf_op jit(solution)/shard_map/ppermute | solution.py:22
  42.4 2.9 %collective-permute-done.8 = bf16[1024,64]{0,1:T(8,128)(2,1)S(1)} collective-permute-done((bf16[1024,64]{0,1:T(8,128)(2,1)S(1)}, bf16[1024,64]{0,1:T(8,128)(2,1)S(1)}, u32[]{:S(2)}, u32[]{:S(2)}) %collective-permute-start.8) | collective-permute-done | bytes 131104 | tf_op jit(solution)/shard_map/ppermute | solution.py:19
  45.3 5.7 %collective-permute-start.11 = (bf16[1024,64]{0,1:T(8,128)(2,1)S(1)}, bf16[1024,64]{0,1:T(8,128)(2,1)S(1)}, u32[]{:S(2)}, u32[]{:S(2)}) collective-permute-start(bf16[1024,64]{0,1:T(8,128)(2,1)S(1)} %collective-permute-done.9), channel_id=1, source_target_pairs={{0,30},{2,0},{4,2},{6,4},{8,6},{10,8},{12,10},{14,12},{16,14},{18,... | collective-permute-start | bytes 393224 | tf_op jit(solution)/shard_map/ppermute | solution.py:22
  51.0 3.1 %collective-permute-done.10 = bf16[1024,64]{0,1:T(8,128)(2,1)S(1)} collective-permute-done((bf16[1024,64]{0,1:T(8,128)(2,1)S(1)}, bf16[1024,64]{0,1:T(8,128)(2,1)S(1)}, u32[]{:S(2)}, u32[]{:S(2)}) %collective-permute-start.10) | collective-permute-done | bytes 131104 | tf_op jit(solution)/shard_map/ppermute | solution.py:19
  54.1 6.1 %collective-permute-start.13 = (bf16[1024,64]{0,1:T(8,128)(2,1)S(1)}, bf16[1024,64]{0,1:T(8,128)(2,1)S(1)}, u32[]{:S(2)}, u32[]{:S(2)}) collective-permute-start(bf16[1024,64]{0,1:T(8,128)(2,1)S(1)} %collective-permute-done.11), channel_id=1, source_target_pairs={{0,30},{2,0},{4,2},{6,4},{8,6},{10,8},{12,10},{14,12},{16,14},{18,... | collective-permute-start | bytes 393224 | tf_op jit(solution)/shard_map/ppermute | solution.py:22
  60.2 3.8 %collective-permute-done.12 = bf16[1024,64]{0,1:T(8,128)(2,1)S(1)} collective-permute-done((bf16[1024,64]{0,1:T(8,128)(2,1)S(1)}, bf16[1024,64]{0,1:T(8,128)(2,1)S(1)}, u32[]{:S(2)}, u32[]{:S(2)}) %collective-permute-start.12) | collective-permute-done | bytes 131104 | tf_op jit(solution)/shard_map/ppermute | solution.py:19
  64.0 8.6 %collective-permute-done.14 = bf16[1024,64]{0,1:T(8,128)(2,1)S(1)} collective-permute-done((bf16[1024,64]{0,1:T(8,128)(2,1)S(1)}, bf16[1024,64]{0,1:T(8,128)(2,1)S(1)}, u32[]{:S(2)}, u32[]{:S(2)}) %collective-permute-start.14) | collective-permute-done | bytes 131104 | tf_op jit(solution)/shard_map/ppermute | solution.py:19
  72.6 1.5 convolution_convert_fusion
  74.2 3.6 %all-to-all-start = ((bf16[16,64,256]{2,1,0:T(8,128)(2,1)}), bf16[16,64,256]{2,1,0:T(8,128)(2,1)S(1)}, u32[]{:S(2)}, u32[]{:S(2)}) async-start(bf16[16,64,256]{2,1,0:T(8,128)(2,1)} %bitcast.1), calls=%async_computation | async-start | bytes 1048576 | tf_op jit(solution)/shard_map/all_to_all | solution.py:71
  78.0 10.5 %all-to-all-done = bf16[16,64,256]{2,1,0:T(8,128)(2,1)S(1)} async-done(((bf16[16,64,256]{2,1,0:T(8,128)(2,1)}), bf16[16,64,256]{2,1,0:T(8,128)(2,1)S(1)}, u32[]{:S(2)}, u32[]{:S(2)}) %all-to-all-start) | async-done | bytes 524320 | tf_op jit(solution)/shard_map/all_to_all | solution.py:71
  88.6 1.3 collective-permute-start.15
  89.9 1.3 collective-permute-start.16
  91.2 1.8 collective-permute-done.16
  93.1 3.1 %gather_fusion = bf16[256,64,128]{2,1,0:T(8,128)(2,1)} fusion(bf16[64,36,128]{2,0,1:T(8,128)(2,1)S(1)} %copy_bitcast_fusion.3, s32[1024]{0:T(1024)S(1)} %pad_clamp_fusion), kind=kCustom, calls=%fused_computation | custom fusion | bytes 8389632 | tf_op jit(solution)/shard_map/gather | solution.py:45
  96.2 7.6 %fusion.12 = f32[32,64,128,1]{2,1,3,0:T(8,128)S(1)} fusion(bf16[64,32,8,128]{3,0,2,1:T(8,128)(2,1)} %bitcast.117, bf16[32,8,128,128]{3,2,1,0:T(8,128)(2,1)} %param.6), kind=kOutput, calls=%fused_computation.52 | convolution fusion | flops 536870912 | bytes 13631488 | tf_op jit(solution)/shard_map/rjab,krjb->kra/dot_general | solution.py:46
  104.0 2.1 %collective-permute-start.17 = (bf16[64,256]{1,0:T(8,128)(2,1)S(1)}, bf16[64,256]{1,0:T(8,128)(2,1)S(1)}, u32[]{:S(2)}, u32[]{:S(2)}) collective-permute-start(bf16[64,256]{1,0:T(8,128)(2,1)S(1)} %get-tuple-element.9), channel_id=1, source_target_pairs={{0,1},{2,3},{4,5},{6,7},{8,9},{10,11},{12,13},{14,15},{16,17},{18,... | collective-permute-start | bytes 98312 | tf_op jit(solution)/shard_map/ppermute | solution.py:34
  106.1 1.3 collective-permute-start.18
  107.4 1.8 collective-permute-done.18
  109.3 3.1 %gather_fusion.1 = bf16[256,64,128]{2,1,0:T(8,128)(2,1)} fusion(bf16[64,36,128]{2,0,1:T(8,128)(2,1)S(1)} %copy_bitcast_fusion.2, s32[1024]{0:T(1024)S(1)} %pad_clamp_fusion), kind=kCustom, calls=%fused_computation.1 | custom fusion | bytes 8389632 | tf_op jit(solution)/shard_map/gather | solution.py:45
  112.4 7.6 %fusion.13 = f32[32,64,128,1]{2,1,3,0:T(8,128)S(1)} fusion(bf16[64,32,8,128]{3,0,2,1:T(8,128)(2,1)} %bitcast.118, bf16[32,8,128,128]{3,2,1,0:T(8,128)(2,1)} %param.6), kind=kOutput, calls=%fused_computation.53 | convolution fusion | flops 536870912 | bytes 13631488 | tf_op jit(solution)/shard_map/rjab,krjb->kra/dot_general | solution.py:46
  120.4 2.1 %collective-permute-start.19 = (bf16[64,256]{1,0:T(8,128)(2,1)S(1)}, bf16[64,256]{1,0:T(8,128)(2,1)S(1)}, u32[]{:S(2)}, u32[]{:S(2)}) collective-permute-start(bf16[64,256]{1,0:T(8,128)(2,1)S(1)} %get-tuple-element.7), channel_id=1, source_target_pairs={{0,1},{2,3},{4,5},{6,7},{8,9},{10,11},{12,13},{14,15},{16,17},{18,... | collective-permute-start | bytes 98312 | tf_op jit(solution)/shard_map/ppermute | solution.py:34
  122.4 1.3 collective-permute-start.20
  123.7 1.8 collective-permute-done.20
  125.7 3.1 %gather_fusion.2 = bf16[256,64,128]{2,1,0:T(8,128)(2,1)} fusion(bf16[64,36,128]{2,0,1:T(8,128)(2,1)S(1)} %copy_bitcast_fusion.1, s32[1024]{0:T(1024)S(1)} %pad_clamp_fusion), kind=kCustom, calls=%fused_computation.2 | custom fusion | bytes 8389632 | tf_op jit(solution)/shard_map/gather | solution.py:45
  128.8 7.6 %fusion.14 = f32[32,64,128,1]{2,1,3,0:T(8,128)S(1)} fusion(bf16[64,32,8,128]{3,0,2,1:T(8,128)(2,1)} %bitcast.119, bf16[32,8,128,128]{3,2,1,0:T(8,128)(2,1)} %param.6), kind=kOutput, calls=%fused_computation.54 | convolution fusion | flops 536870912 | bytes 13631488 | tf_op jit(solution)/shard_map/rjab,krjb->kra/dot_general | solution.py:46
  138.2 2.1 %collective-permute-start.21 = (bf16[64,256]{1,0:T(8,128)(2,1)S(1)}, bf16[64,256]{1,0:T(8,128)(2,1)S(1)}, u32[]{:S(2)}, u32[]{:S(2)}) collective-permute-start(bf16[64,256]{1,0:T(8,128)(2,1)S(1)} %get-tuple-element.5), channel_id=1, source_target_pairs={{0,1},{2,3},{4,5},{6,7},{8,9},{10,11},{12,13},{14,15},{16,17},{18,... | collective-permute-start | bytes 98312 | tf_op jit(solution)/shard_map/ppermute | solution.py:34
  140.3 1.5 collective-permute-start.22
  141.8 1.6 copy.24
  143.3 2.5 %reshape.50 = f32[64,16,256]{2,1,0:T(8,128)} reshape(f32[64,32,128]{2,1,0:T(8,128)} %copy.24) | data formatting | bytes 2097152 | tf_op jit(solution)/shard_map/reshape | solution.py:47
  145.9 1.6 copy.26
  147.4 1.5 reshape.49
  149.0 1.6 copy.28
  150.6 2.5 %reshape.48 = f32[64,16,256]{2,1,0:T(8,128)} reshape(f32[64,32,128]{2,1,0:T(8,128)} %copy.28) | data formatting | bytes 2097152 | tf_op jit(solution)/shard_map/reshape | solution.py:47
  153.3 3.1 %gather_fusion.3 = bf16[256,64,128]{2,1,0:T(8,128)(2,1)} fusion(bf16[64,36,128]{2,0,1:T(8,128)(2,1)S(1)} %copy_bitcast_fusion, s32[1024]{0:T(1024)S(1)} %pad_clamp_fusion), kind=kCustom, calls=%fused_computation.3 | custom fusion | bytes 8389632 | tf_op jit(solution)/shard_map/gather | solution.py:45
  156.4 7.6 %convolution_bitcast_fusion = f32[64,32,128]{2,0,1:T(8,128)S(1)} fusion(bf16[64,32,8,128]{3,0,2,1:T(8,128)(2,1)} %bitcast.116, bf16[32,8,128,128]{3,2,1,0:T(8,128)(2,1)} %param.6), kind=kOutput, calls=%fused_computation.4 | convolution fusion | flops 536870912 | bytes 13631488 | tf_op jit(solution)/shard_map/rjab,krjb->kra/dot_general | solution.py:46
  164.0 1.6 copy.30
  165.6 2.5 %reshape.47 = f32[64,16,256]{2,1,0:T(8,128)} reshape(f32[64,32,128]{2,1,0:T(8,128)} %copy.30) | data formatting | bytes 2097152 | tf_op jit(solution)/shard_map/reshape | solution.py:47
  168.1 2.4 %subtract_convert_fusion = bf16[64,16,256]{2,1,0:T(8,128)(2,1)S(1)} fusion(f32[64,16,256]{2,1,0:T(8,128)} %reshape.47, f32[64,16,256]{2,1,0:T(8,128)} %reshape.48, f32[64,16,256]{2,1,0:T(8,128)S(1)} %reshape.49, f32[64,16,256]{2,1,0:T(8,128)S(1)} %copy-done.8, bf16[16,64,256]{2,1,0:T(8,128)(2,1)S(1)} %copy-done.7), kind=kLoop, calls=%fused_computation.18 | loop fusion | flops 4456448 | bytes 5242880 | tf_op jit(solution)/shard_map/convert_element_type | solution.py:61
  170.6 19.1 %all_to_all.35 = bf16[64,16,256]{2,0,1:T(8,128)(2,1)S(1)} all-to-all(bf16[64,16,256]{2,0,1:T(8,128)(2,1)S(1)} %copy.34), channel_id=1, replica_groups=mesh['vec'=16,'row'=2] {'vec'}, dimensions={1} | all-to-all | bytes 1048576 | tf_op jit(solution)/shard_map/all_to_all | solution.py:73
  (80 shorter events, 5.0 us)
Async XLA Ops:
  0.0 72.6 %copy-start = (bf16[1,256,1024]{2,1,0:T(8,128)(2,1)S(1)}, bf16[1,256,1024]{2,1,0:T(8,128)(2,1)}, u32[]{:S(2)}) copy-start(bf16[1,256,1024]{2,1,0:T(8,128)(2,1)} %param.4) | copy-start | bytes 1572868
  0.0 7.3 %copy-start.11 = (bf16[1024,64]{0,1:T(8,128)(2,1)S(1)}, bf16[1024,64]{0,1:T(8,128)(2,1)}, u32[]{:S(2)}) copy-start(bf16[1024,64]{0,1:T(8,128)(2,1)} %param.5) | copy-start | bytes 393220
  0.0 10.8 %collective-permute-start = (bf16[1024,64]{0,1:T(8,128)(2,1)}, bf16[1024,64]{0,1:T(8,128)(2,1)S(1)}, u32[]{:S(2)}, u32[]{:S(2)}) collective-permute-start(bf16[1024,64]{0,1:T(8,128)(2,1)} %param.5), channel_id=1, source_target_pairs={{0,2},{2,4},{4,6},{6,8},{8,10},{10,12},{12,14},{14,16},{16,18},{18... | collective-permute-start | bytes 393224 | tf_op jit(solution)/shard_map/ppermute | solution.py:19
  3.0 8.1 %collective-permute-start.1 = (bf16[1024,64]{0,1:T(8,128)(2,1)}, bf16[1024,64]{0,1:T(8,128)(2,1)S(1)}, u32[]{:S(2)}, u32[]{:S(2)}) collective-permute-start(bf16[1024,64]{0,1:T(8,128)(2,1)} %param.5), channel_id=1, source_target_pairs={{0,30},{2,0},{4,2},{6,4},{8,6},{10,8},{12,10},{14,12},{16,14},{18,... | collective-permute-start | bytes 393224 | tf_op jit(solution)/shard_map/ppermute | solution.py:22
  10.8 8.6 %collective-permute-start.2 = (bf16[1024,64]{0,1:T(8,128)(2,1)S(1)}, bf16[1024,64]{0,1:T(8,128)(2,1)S(1)}, u32[]{:S(2)}, u32[]{:S(2)}) collective-permute-start(bf16[1024,64]{0,1:T(8,128)(2,1)S(1)} %collective-permute-done), channel_id=1, source_target_pairs={{0,2},{2,4},{4,6},{6,8},{8,10},{10,12},{12,14},{14,16},{16,18},{18... | collective-permute-start | bytes 393224 | tf_op jit(solution)/shard_map/ppermute | solution.py:19
  11.0 8.3 %collective-permute-start.3 = (bf16[1024,64]{0,1:T(8,128)(2,1)S(1)}, bf16[1024,64]{0,1:T(8,128)(2,1)S(1)}, u32[]{:S(2)}, u32[]{:S(2)}) collective-permute-start(bf16[1024,64]{0,1:T(8,128)(2,1)S(1)} %collective-permute-done.1), channel_id=1, source_target_pairs={{0,30},{2,0},{4,2},{6,4},{8,6},{10,8},{12,10},{14,12},{16,14},{18,... | collective-permute-start | bytes 393224 | tf_op jit(solution)/shard_map/ppermute | solution.py:22
  19.4 8.7 %collective-permute-start.4 = (bf16[1024,64]{0,1:T(8,128)(2,1)S(1)}, bf16[1024,64]{0,1:T(8,128)(2,1)S(1)}, u32[]{:S(2)}, u32[]{:S(2)}) collective-permute-start(bf16[1024,64]{0,1:T(8,128)(2,1)S(1)} %collective-permute-done.2), channel_id=1, source_target_pairs={{0,2},{2,4},{4,6},{6,8},{8,10},{10,12},{12,14},{14,16},{16,18},{18... | collective-permute-start | bytes 393224 | tf_op jit(solution)/shard_map/ppermute | solution.py:19
  19.4 8.7 %collective-permute-start.5 = (bf16[1024,64]{0,1:T(8,128)(2,1)S(1)}, bf16[1024,64]{0,1:T(8,128)(2,1)S(1)}, u32[]{:S(2)}, u32[]{:S(2)}) collective-permute-start(bf16[1024,64]{0,1:T(8,128)(2,1)S(1)} %collective-permute-done.3), channel_id=1, source_target_pairs={{0,30},{2,0},{4,2},{6,4},{8,6},{10,8},{12,10},{14,12},{16,14},{18,... | collective-permute-start | bytes 393224 | tf_op jit(solution)/shard_map/ppermute | solution.py:22
  28.0 8.7 %collective-permute-start.6 = (bf16[1024,64]{0,1:T(8,128)(2,1)S(1)}, bf16[1024,64]{0,1:T(8,128)(2,1)S(1)}, u32[]{:S(2)}, u32[]{:S(2)}) collective-permute-start(bf16[1024,64]{0,1:T(8,128)(2,1)S(1)} %collective-permute-done.4), channel_id=1, source_target_pairs={{0,2},{2,4},{4,6},{6,8},{8,10},{10,12},{12,14},{14,16},{16,18},{18... | collective-permute-start | bytes 393224 | tf_op jit(solution)/shard_map/ppermute | solution.py:19
  28.0 8.7 %collective-permute-start.7 = (bf16[1024,64]{0,1:T(8,128)(2,1)S(1)}, bf16[1024,64]{0,1:T(8,128)(2,1)S(1)}, u32[]{:S(2)}, u32[]{:S(2)}) collective-permute-start(bf16[1024,64]{0,1:T(8,128)(2,1)S(1)} %collective-permute-done.5), channel_id=1, source_target_pairs={{0,30},{2,0},{4,2},{6,4},{8,6},{10,8},{12,10},{14,12},{16,14},{18,... | collective-permute-start | bytes 393224 | tf_op jit(solution)/shard_map/ppermute | solution.py:22
  36.7 8.6 %collective-permute-start.8 = (bf16[1024,64]{0,1:T(8,128)(2,1)S(1)}, bf16[1024,64]{0,1:T(8,128)(2,1)S(1)}, u32[]{:S(2)}, u32[]{:S(2)}) collective-permute-start(bf16[1024,64]{0,1:T(8,128)(2,1)S(1)} %collective-permute-done.6), channel_id=1, source_target_pairs={{0,2},{2,4},{4,6},{6,8},{8,10},{10,12},{12,14},{14,16},{16,18},{18... | collective-permute-start | bytes 393224 | tf_op jit(solution)/shard_map/ppermute | solution.py:19
  36.7 8.6 %collective-permute-start.9 = (bf16[1024,64]{0,1:T(8,128)(2,1)S(1)}, bf16[1024,64]{0,1:T(8,128)(2,1)S(1)}, u32[]{:S(2)}, u32[]{:S(2)}) collective-permute-start(bf16[1024,64]{0,1:T(8,128)(2,1)S(1)} %collective-permute-done.7), channel_id=1, source_target_pairs={{0,30},{2,0},{4,2},{6,4},{8,6},{10,8},{12,10},{14,12},{16,14},{18,... | collective-permute-start | bytes 393224 | tf_op jit(solution)/shard_map/ppermute | solution.py:22
  45.3 8.8 %collective-permute-start.10 = (bf16[1024,64]{0,1:T(8,128)(2,1)S(1)}, bf16[1024,64]{0,1:T(8,128)(2,1)S(1)}, u32[]{:S(2)}, u32[]{:S(2)}) collective-permute-start(bf16[1024,64]{0,1:T(8,128)(2,1)S(1)} %collective-permute-done.8), channel_id=1, source_target_pairs={{0,2},{2,4},{4,6},{6,8},{8,10},{10,12},{12,14},{14,16},{16,18},{18... | collective-permute-start | bytes 393224 | tf_op jit(solution)/shard_map/ppermute | solution.py:19
  45.3 8.8 %collective-permute-start.11 = (bf16[1024,64]{0,1:T(8,128)(2,1)S(1)}, bf16[1024,64]{0,1:T(8,128)(2,1)S(1)}, u32[]{:S(2)}, u32[]{:S(2)}) collective-permute-start(bf16[1024,64]{0,1:T(8,128)(2,1)S(1)} %collective-permute-done.9), channel_id=1, source_target_pairs={{0,30},{2,0},{4,2},{6,4},{8,6},{10,8},{12,10},{14,12},{16,14},{18,... | collective-permute-start | bytes 393224 | tf_op jit(solution)/shard_map/ppermute | solution.py:22
  54.1 9.9 %collective-permute-start.12 = (bf16[1024,64]{0,1:T(8,128)(2,1)S(1)}, bf16[1024,64]{0,1:T(8,128)(2,1)S(1)}, u32[]{:S(2)}, u32[]{:S(2)}) collective-permute-start(bf16[1024,64]{0,1:T(8,128)(2,1)S(1)} %collective-permute-done.10), channel_id=1, source_target_pairs={{0,2},{2,4},{4,6},{6,8},{8,10},{10,12},{12,14},{14,16},{16,18},{18... | collective-permute-start | bytes 393224 | tf_op jit(solution)/shard_map/ppermute | solution.py:19
  54.1 9.9 %collective-permute-start.13 = (bf16[1024,64]{0,1:T(8,128)(2,1)S(1)}, bf16[1024,64]{0,1:T(8,128)(2,1)S(1)}, u32[]{:S(2)}, u32[]{:S(2)}) collective-permute-start(bf16[1024,64]{0,1:T(8,128)(2,1)S(1)} %collective-permute-done.11), channel_id=1, source_target_pairs={{0,30},{2,0},{4,2},{6,4},{8,6},{10,8},{12,10},{14,12},{16,14},{18,... | collective-permute-start | bytes 393224 | tf_op jit(solution)/shard_map/ppermute | solution.py:22
  64.0 8.6 %collective-permute-start.14 = (bf16[1024,64]{0,1:T(8,128)(2,1)S(1)}, bf16[1024,64]{0,1:T(8,128)(2,1)S(1)}, u32[]{:S(2)}, u32[]{:S(2)}) collective-permute-start(bf16[1024,64]{0,1:T(8,128)(2,1)S(1)} %collective-permute-done.12), channel_id=1, source_target_pairs={{0,2},{2,4},{4,6},{6,8},{8,10},{10,12},{12,14},{14,16},{16,18},{18... | collective-permute-start | bytes 393224 | tf_op jit(solution)/shard_map/ppermute | solution.py:19
  72.6 5.1 %copy-start.12 = (s32[32,8]{0,1:T(8,128)S(1)}, s32[32,8]{0,1:T(8,128)}, u32[]{:S(2)}) copy-start(s32[32,8]{0,1:T(8,128)} %param.7) | copy-start | bytes 3076
  74.2 14.3 %all-to-all-start = ((bf16[16,64,256]{2,1,0:T(8,128)(2,1)}), bf16[16,64,256]{2,1,0:T(8,128)(2,1)S(1)}, u32[]{:S(2)}, u32[]{:S(2)}) async-start(bf16[16,64,256]{2,1,0:T(8,128)(2,1)} %bitcast.1), calls=%async_computation | async-start | bytes 1048576 | tf_op jit(solution)/shard_map/all_to_all | solution.py:71
  88.5 2.7 %copy-start.6 = (bf16[16,64,256]{2,1,0:T(8,128)(2,1)}, bf16[16,64,256]{2,1,0:T(8,128)(2,1)S(1)}, u32[]{:S(2)}) copy-start(bf16[16,64,256]{2,1,0:T(8,128)(2,1)S(1)} %all-to-all-done) | copy-start | bytes 1572868
  88.5 15.3 %copy-start.1 = (bf16[8,8,16,256]{3,1,2,0:T(8,128)(2,1)}, bf16[8,8,16,256]{3,1,2,0:T(8,128)(2,1)S(1)}, u32[]{:S(2)}) copy-start(bf16[8,8,16,256]{3,1,2,0:T(8,128)(2,1)S(1)} %copy.47) | copy-start | bytes 1572868
  88.6 2.6 %collective-permute-start.15 = (bf16[64,256]{1,0:T(8,128)(2,1)S(1)}, bf16[64,256]{1,0:T(8,128)(2,1)S(1)}, u32[]{:S(2)}, u32[]{:S(2)}) collective-permute-start(bf16[64,256]{1,0:T(8,128)(2,1)S(1)} %get-tuple-element.11), channel_id=1, source_target_pairs={{0,1},{2,3},{4,5},{6,7},{8,9},{10,11},{12,13},{14,15},{16,17},{18,... | collective-permute-start | bytes 98312 | tf_op jit(solution)/shard_map/ppermute | solution.py:34
  89.9 3.1 %collective-permute-start.16 = (bf16[64,256]{1,0:T(8,128)(2,1)S(1)}, bf16[64,256]{1,0:T(8,128)(2,1)S(1)}, u32[]{:S(2)}, u32[]{:S(2)}) collective-permute-start(bf16[64,256]{1,0:T(8,128)(2,1)S(1)} %get-tuple-element.12), channel_id=1, source_target_pairs={{1,0},{3,2},{5,4},{7,6},{9,8},{11,10},{13,12},{15,14},{17,16},{19,... | collective-permute-start | bytes 98312 | tf_op jit(solution)/shard_map/ppermute | solution.py:37
  104.0 3.4 %collective-permute-start.17 = (bf16[64,256]{1,0:T(8,128)(2,1)S(1)}, bf16[64,256]{1,0:T(8,128)(2,1)S(1)}, u32[]{:S(2)}, u32[]{:S(2)}) collective-permute-start(bf16[64,256]{1,0:T(8,128)(2,1)S(1)} %get-tuple-element.9), channel_id=1, source_target_pairs={{0,1},{2,3},{4,5},{6,7},{8,9},{10,11},{12,13},{14,15},{16,17},{18,... | collective-permute-start | bytes 98312 | tf_op jit(solution)/shard_map/ppermute | solution.py:34
  106.1 3.1 %collective-permute-start.18 = (bf16[64,256]{1,0:T(8,128)(2,1)S(1)}, bf16[64,256]{1,0:T(8,128)(2,1)S(1)}, u32[]{:S(2)}, u32[]{:S(2)}) collective-permute-start(bf16[64,256]{1,0:T(8,128)(2,1)S(1)} %get-tuple-element.10), channel_id=1, source_target_pairs={{1,0},{3,2},{5,4},{7,6},{9,8},{11,10},{13,12},{15,14},{17,16},{19,... | collective-permute-start | bytes 98312 | tf_op jit(solution)/shard_map/ppermute | solution.py:37
  112.4 7.7 %copy-start.2 = (bf16[8,8,16,256]{3,1,2,0:T(8,128)(2,1)S(1)}, bf16[8,8,16,256]{3,1,2,0:T(8,128)(2,1)}, u32[]{:S(2)}) copy-start(bf16[8,8,16,256]{3,1,2,0:T(8,128)(2,1)} %copy-done.1) | copy-start | bytes 1572868
  120.4 3.4 %collective-permute-start.19 = (bf16[64,256]{1,0:T(8,128)(2,1)S(1)}, bf16[64,256]{1,0:T(8,128)(2,1)S(1)}, u32[]{:S(2)}, u32[]{:S(2)}) collective-permute-start(bf16[64,256]{1,0:T(8,128)(2,1)S(1)} %get-tuple-element.7), channel_id=1, source_target_pairs={{0,1},{2,3},{4,5},{6,7},{8,9},{10,11},{12,13},{14,15},{16,17},{18,... | collective-permute-start | bytes 98312 | tf_op jit(solution)/shard_map/ppermute | solution.py:34
  122.4 3.1 %collective-permute-start.20 = (bf16[64,256]{1,0:T(8,128)(2,1)S(1)}, bf16[64,256]{1,0:T(8,128)(2,1)S(1)}, u32[]{:S(2)}, u32[]{:S(2)}) collective-permute-start(bf16[64,256]{1,0:T(8,128)(2,1)S(1)} %get-tuple-element.8), channel_id=1, source_target_pairs={{1,0},{3,2},{5,4},{7,6},{9,8},{11,10},{13,12},{15,14},{17,16},{19,... | collective-permute-start | bytes 98312 | tf_op jit(solution)/shard_map/ppermute | solution.py:37
  128.8 7.7 %copy-start.3 = (bf16[8,8,16,256]{3,1,2,0:T(8,128)(2,1)S(1)}, bf16[8,8,16,256]{3,1,2,0:T(8,128)(2,1)}, u32[]{:S(2)}) copy-start(bf16[8,8,16,256]{3,1,2,0:T(8,128)(2,1)} %copy-done.1) | copy-start | bytes 1572868
  136.4 1.0 copy-start.4
  137.4 0.8 copy-start.9
  138.2 14.9 %collective-permute-start.21 = (bf16[64,256]{1,0:T(8,128)(2,1)S(1)}, bf16[64,256]{1,0:T(8,128)(2,1)S(1)}, u32[]{:S(2)}, u32[]{:S(2)}) collective-permute-start(bf16[64,256]{1,0:T(8,128)(2,1)S(1)} %get-tuple-element.5), channel_id=1, source_target_pairs={{0,1},{2,3},{4,5},{6,7},{8,9},{10,11},{12,13},{14,15},{16,17},{18,... | collective-permute-start | bytes 98312 | tf_op jit(solution)/shard_map/ppermute | solution.py:34
  140.3 12.9 %collective-permute-start.22 = (bf16[64,256]{1,0:T(8,128)(2,1)S(1)}, bf16[64,256]{1,0:T(8,128)(2,1)S(1)}, u32[]{:S(2)}, u32[]{:S(2)}) collective-permute-start(bf16[64,256]{1,0:T(8,128)(2,1)S(1)} %get-tuple-element.6), channel_id=1, source_target_pairs={{1,0},{3,2},{5,4},{7,6},{9,8},{11,10},{13,12},{15,14},{17,16},{19,... | collective-permute-start | bytes 98312 | tf_op jit(solution)/shard_map/ppermute | solution.py:37
  145.9 3.1 %copy-start.5 = (f32[32,64,128,1]{2,1,3,0:T(8,128)S(1)}, f32[32,64,128,1]{2,1,3,0:T(8,128)}, u32[]{:S(2)}) copy-start(f32[32,64,128,1]{2,1,3,0:T(8,128)} %copy-done.4) | copy-start | bytes 3145732
  149.0 4.1 %copy-start.10 = (bf16[64,4096]{1,0:T(8,128)(2,1)S(1)}, bf16[64,4096]{1,0:T(8,128)(2,1)}, u32[]{:S(2)}) copy-start(bf16[64,4096]{1,0:T(8,128)(2,1)} %copy-done.9) | copy-start | bytes 1572868
  164.0 4.1 %copy-start.7 = (bf16[16,64,256]{2,1,0:T(8,128)(2,1)S(1)}, bf16[16,64,256]{2,1,0:T(8,128)(2,1)}, u32[]{:S(2)}) copy-start(bf16[16,64,256]{2,1,0:T(8,128)(2,1)} %copy-done.6) | copy-start | bytes 1572868
  164.0 4.1 %copy-start.8 = (f32[64,16,256]{2,1,0:T(8,128)S(1)}, f32[64,16,256]{2,1,0:T(8,128)}, u32[]{:S(2)}) copy-start(f32[64,16,256]{2,1,0:T(8,128)} %reshape.50) | copy-start | bytes 3145732
